TPU v7x, 512 devices: a whole 4x4x16 slice. The times are simulated.
512 devices in a mesh: dp: 64 (over y_lo, z, core), mp: 8 (over y_hi, x).
Axes of the slice: x: 4, y: 4 (y_hi: 2, y_lo: 2; y = y_hi * 2 + y_lo), z: 16, core: 2. Of those that a mesh axis runs over, the one named last changes fastest.
Arguments:
- acts: bfloat16 [16384, 28672], P('dp', 'mp'), may hold values from -24 to 24
- grads: bfloat16 [16384, 8192], P('dp', 'mp'), may hold values from -6 to 6
- basis_in: bfloat16 [28672, 640], P('mp', 'dp'), may hold values from -0.03125 to 0.03125
- basis_out: bfloat16 [8192, 1024], P('dp', 'mp'), may hold values from -0.0625 to 0.0625
- damping: float32 [1], replicated, may hold values from 0.5 to 2
Outputs:
- update: bfloat16 [28672, 8192], P('mp', 'dp')
- diag: float32 [640, 1024], P('mp', 'dp')
All inputs are finite; a program needn't handle non-finite values.
Results may differ from a plain program's by a relative error of at most 0.0085.
Values may be sent and summed in bfloat16 or wider, within the bound.
A program may use at most 64 MiB of HBM per device.

v0:
```python
import jax
import jax.numpy as jnp
from jax import lax
from jax.sharding import PartitionSpec as P


def on_device(acts, grads, basis_in, basis_out, damping):
    tok_rows = acts.shape[0]
    tokens_all = tok_rows * lax.axis_size("dp")
    whole_grads = lax.all_gather(grads, "mp", axis=1, tiled=True)
    grad_proj = jnp.dot(
        whole_grads,
        lax.all_gather(basis_out, "dp", axis=0, tiled=True),
        preferred_element_type=jnp.float32,
    ).astype(jnp.bfloat16)
    full_in = lax.all_gather(basis_in, "dp", axis=1, tiled=True)
    act_proj_t = lax.psum_scatter(
        lax.dot_general(
            full_in, acts, (((0,), (1,)), ((), ())), preferred_element_type=jnp.float32
        ),
        "mp",
        scatter_dimension=0,
        tiled=True,
    ).astype(jnp.bfloat16)
    act_sq_t = (act_proj_t.astype(jnp.float32) ** 2).astype(jnp.bfloat16)
    grad_sq = (grad_proj.astype(jnp.float32) ** 2).astype(jnp.bfloat16)
    stacked = jnp.stack([grad_proj, grad_sq])
    piece = lax.all_gather(stacked, "mp", axis=2, tiled=True)
    rotated = jnp.dot(act_proj_t, piece[0], preferred_element_type=jnp.float32)
    squares = jnp.dot(act_sq_t, piece[1], preferred_element_type=jnp.float32)
    partials = jnp.stack([rotated, squares])
    owned = lax.psum_scatter(partials, "dp", scatter_dimension=2, tiled=True)
    diag = owned[1] / tokens_all
    scaled = (owned[0] / (diag + damping[0])).astype(jnp.bfloat16)
    out_rows = lax.all_gather(basis_out, "mp", axis=1, tiled=True)
    dims = (((1,), (1,)), ((), ()))
    scaled_wide = lax.all_gather(scaled, "dp", axis=1, tiled=True)
    scaled_full = lax.all_gather(scaled_wide, "mp", axis=0, tiled=True)
    back = lax.dot_general(scaled_full, out_rows, dims, preferred_element_type=jnp.float32).astype(
        jnp.bfloat16
    )
    update = jnp.dot(full_in, back, preferred_element_type=jnp.float32)
    return (update.astype(jnp.bfloat16), diag)


def solution(mesh):
    placed = (P("dp", "mp"), P("dp", "mp"), P("mp", "dp"), P("dp", "mp"), P())
    return jax.shard_map(
        on_device,
        mesh=mesh,
        in_specs=placed,
        out_specs=(P("mp", "dp"), P("mp", "dp")),
        check_vma=False,
    )
```

profile of v0, /device:TPU:2, one launch (start us, length us, event | category | flops | bytes accessed | tf_op | source)
XLA Modules:
  0.0 1079.5 jit_solution(1085636390495247304)
XLA Ops:
  7.2 0.0 all-gather.9.cloned.1.call-start
  7.2 0.7 all-gather.9.cloned.1.call-update
  7.9 0.0 all-gather.7.cloned.1.call-start
  8.0 0.7 all-gather.7.cloned.1.call-update
  8.7 0.0 all-gather.15.cloned.1.call-start
  8.7 0.7 all-gather.15.cloned.1.call-update
  9.4 0.0 all-gather.11.cloned.1.call-start
  9.4 127.1 %all-gather.9.cloned.1.call-done = bf16[8192,128]{1,0:T(8,128)(2,1)} async-done(((bf16[128,128]{1,0:T(8,128)(2,1)}), bf16[8192,128]{1,0:T(8,128)(2,1)}) %all-gather.9.cloned.1.call-update) | async-done | bytes 2097168 | tf_op jit(solution)/shard_map/all_gather | solution.py:13
  136.6 85.5 %all-gather.7.cloned.1.call-done = bf16[256,8192]{1,0:T(8,128)(2,1)} async-done(((bf16[256,1024]{1,0:T(8,128)(2,1)}), bf16[256,8192]{1,0:T(8,128)(2,1)}) %all-gather.7.cloned.1.call-update) | async-done | bytes 4194320 | tf_op jit(solution)/shard_map/all_gather | solution.py:10
  222.1 4.1 convolution_convert_fusion.2
  226.2 0.7 pad_maximum_fusion.1
  226.9 0.0 reduce-scatter.2.cloned.1.call-start
  227.0 123.7 %all-gather.15.cloned.1.call-done = bf16[64,10,3584]{2,1,0:T(8,128)(2,1)} async-done(((bf16[1,10,3584]{2,1,0:T(8,128)(2,1)}), bf16[64,10,3584]{2,1,0:T(8,128)(2,1)}) %all-gather.15.cloned.1.call-update) | async-done | bytes 4587536 | tf_op jit(solution)/shard_map/all_gather | solution.py:16
  350.6 8.0 reshape.7
  358.6 4.5 fusion.4
  363.2 0.0 all-reduce.3.cloned.1.call-start
  363.2 50.1 %all-gather.11.cloned.1.call-done = bf16[2,256,1024]{2,1,0:T(8,128)(2,1)} async-done(((bf16[2,256,128]{2,1,0:T(8,128)(2,1)}), bf16[2,256,1024]{2,1,0:T(8,128)(2,1)}) %all-gather.11.cloned.1.call-update) | async-done | bytes 1048592 | tf_op jit(solution)/shard_map/all_gather | solution.py:28
  413.3 91.6 %reduce-scatter.2.cloned.1.call-done = f32[80,256]{1,0:T(8,128)} async-done(((f32[640,256]{1,0:T(8,128)}), f32[80,256]{1,0:T(8,128)}) %reduce-scatter.2.cloned.1.call-update) | async-done | bytes 81936 | tf_op jit(solution)/shard_map/reduce_scatter | solution.py:17
  504.9 1.3 convolution_bitcast_fusion
  506.2 1.3 convolution_bitcast_fusion.1
  507.5 0.1 pad_maximum_fusion
  507.5 1.3 copy.14
  508.9 0.0 all-gather.13.cloned.1.call-start
  509.6 1.3 dynamic-slice
  511.5 435.9 %all-reduce.3.cloned.1.call-done = f32[2,80,1024]{1,0,2:T(2,128)} async-done(((f32[2,80,1024]{1,0,2:T(2,128)}), f32[2,80,1024]{1,0,2:T(2,128)}) %all-reduce.3.cloned.1.call-update) | async-done | bytes 655376
  947.4 0.8 dynamic-slice_multiply_fusion
  948.2 62.7 %all_gather.25 = bf16[80,1024]{0,1:T(8,128)(2,1)S(1)} all-gather(bf16[80,16]{0,1:T(8,128)(2,1)S(1)} %divide_convert_fusion), channel_id=1, replica_groups=mesh['dp'=64,'mp'=8] {'dp'}, dimensions={1}, use_global_device_ids=true | all-gather | bytes 166400 | tf_op jit(solution)/shard_map/all_gather | solution.py:37
  1010.9 0.8 copy.16
  1011.7 30.1 %all_gather.27 = bf16[128,1024]{1,0:T(8,128)(2,1)S(1)} all-gather(bf16[128,128]{1,0:T(8,128)(2,1)S(1)} %copy-done.1), channel_id=1, replica_groups=mesh['dp'=64,'mp'=8] {'mp'}, dimensions={1}, use_global_device_ids=true | all-gather | bytes 294912 | tf_op jit(solution)/shard_map/all_gather | solution.py:35
  1041.8 24.9 %all-gather.13.cloned.1.call-done = bf16[640,1024]{1,0:T(8,128)(2,1)} async-done(((bf16[80,1024]{1,0:T(8,128)(2,1)}), bf16[640,1024]{1,0:T(8,128)(2,1)}) %all-gather.13.cloned.1.call-update) | async-done | bytes 1310736 | tf_op jit(solution)/shard_map/all_gather | solution.py:38
  1066.7 4.7 fusion
  1071.4 1.3 copy.17
  (12 shorter events, 0.1 us)
Async XLA Ops:
  7.2 351.5 %copy-start = (bf16[256,3584]{1,0:T(8,128)(2,1)S(1)}, bf16[256,3584]{1,0:T(8,128)(2,1)}, u32[]{:S(2)}) copy-start(bf16[256,3584]{1,0:T(8,128)(2,1)} %param.5) | copy-start | bytes 5505028
  7.2 129.4 %all-gather.9.cloned.1.call-start = ((), (), s32[]{:S(2)}) async-start(), calls=%async_computation.3 | async-start | bytes 2129920 | tf_op jit(solution)/shard_map/all_gather | solution.py:13
  7.9 214.2 %all-gather.7.cloned.1.call-start = ((), (), s32[]{:S(2)}) async-start(), calls=%async_computation.2 | async-start | bytes 4718592 | tf_op jit(solution)/shard_map/all_gather | solution.py:10
  8.7 342.0 %all-gather.15.cloned.1.call-start = ((), (), s32[]{:S(2)}) async-start(), calls=%async_computation.6 | async-start | bytes 7454720 | tf_op jit(solution)/shard_map/all_gather | solution.py:16
  9.4 403.9 %all-gather.11.cloned.1.call-start = ((), (), s32[]{:S(2)}) async-start(), calls=%async_computation.4 | async-start | bytes 1179648 | tf_op jit(solution)/shard_map/all_gather | solution.py:28
  226.9 277.9 %reduce-scatter.2.cloned.1.call-start = ((), (), s32[]{:S(2)}) async-start(), calls=%async_computation.1 | async-start | bytes 737280 | tf_op jit(solution)/shard_map/reduce_scatter | solution.py:17
  363.2 584.2 %all-reduce.3.cloned.1.call-start = ((), (), s32[]{:S(2)}) async-start(), calls=%async_computation.7 | async-start | bytes 2097152
  507.5 504.2 %copy-start.1 = (bf16[128,128]{1,0:T(8,128)(2,1)S(1)}, bf16[128,128]{1,0:T(8,128)(2,1)}, u32[]{:S(2)}) copy-start(bf16[128,128]{1,0:T(8,128)(2,1)} %param.8) | copy-start | bytes 98308
  508.9 557.8 %all-gather.13.cloned.1.call-start = ((), (), s32[]{:S(2)}) async-start(), calls=%async_computation.5 | async-start | bytes 1474560 | tf_op jit(solution)/shard_map/all_gather | solution.py:38
  948.2 123.2 %copy-start.2 = (f32[1,80,16]{1,0,2:T(1,128)}, f32[1,80,16]{1,0,2:T(1,128)S(1)}, u32[]{:S(2)}) copy-start(f32[1,80,16]{1,0,2:T(1,128)S(1)} %get-tuple-element.10) | copy-start | bytes 15364
Sparse Core Ops, SparseCore 0:
  10.1 126.3 all-gather.8
  139.8 82.2 all-gather.6
  224.3 126.3 all-gather.14
  353.5 59.7 all-gather.10
  418.2 86.6 reduce-scatter.1
  509.0 438.3 all-reduce.2
  1011.9 54.7 all-gather.12
where the time goes:
time: 1080 us
  waiting for transfers between devices  941 us (87%)
  blocking collectives  92.8 us (9%)
  matrix products  15.9 us (1%)
  between operations  15.5 us (1%)
  local copies, waits for them, and re-layouts  12.7 us (1%)
    unnamed x8, waiting for transfers between devices  438 us
    all_gather x1, waiting for transfers between devices, on_device(): lax.all_gather(basis_out, 'dp', axis=0, tiled=True)  127 us
    all_gather x1, waiting for transfers between devices, on_device(): full_in = lax.all_gather(basis_in, 'dp', axis=1, tiled=True)  124 us
    reduce_scatter x1, waiting for transfers between devices, on_device(): lax.psum_scatter(lax.dot_general(full_in, acts, (((0,), (1,)), ((), ())),...  91.6 us
    all_gather x1, waiting for transfers between devices, on_device(): whole_grads = lax.all_gather(grads, 'mp', axis=1, tiled=True)  85.5 us
    all_gather x1, blocking collectives, on_device(): scaled_wide = lax.all_gather(scaled, 'dp', axis=1, tiled=True)  62.7 us
    all_gather x1, waiting for transfers between devices, on_device(): piece = lax.all_gather(stacked, 'mp', axis=2, tiled=True)  50.1 us
    all_gather x1, blocking collectives, on_device(): out_rows = lax.all_gather(basis_out, 'mp', axis=1, tiled=True)  30.1 us
  transfers between devices with their start and end apart: 7, of which 7 were waited for; matrix products, arithmetic and copies ran while one was open for 2% of the time, Pallas kernels for 0%

commit v1 on v0

--- a/solution.py
+++ b/solution.py
@@ -2,6 +2,11 @@
 import jax.numpy as jnp
 from jax import lax
 from jax.sharding import PartitionSpec as P
+
+
+def swapped_in(x, name, dim):
+    repeated = jnp.stack([x] * lax.axis_size(name))
+    return jnp.concatenate(lax.all_to_all(repeated, name, 0, 0), axis=dim)
 
 
 def on_device(acts, grads, basis_in, basis_out, damping):
@@ -9,9 +14,7 @@
     tokens_all = tok_rows * lax.axis_size("dp")
     whole_grads = lax.all_gather(grads, "mp", axis=1, tiled=True)
     grad_proj = jnp.dot(
-        whole_grads,
-        lax.all_gather(basis_out, "dp", axis=0, tiled=True),
-        preferred_element_type=jnp.float32,
+        whole_grads, swapped_in(basis_out, "dp", 0), preferred_element_type=jnp.float32
     ).astype(jnp.bfloat16)
     full_in = lax.all_gather(basis_in, "dp", axis=1, tiled=True)
     act_proj_t = lax.psum_scatter(

time: 1080 us -> 967 us (0.90)
  waiting for transfers between devices: 941 us -> 808 us
  starting transfers between devices: 0.28 us -> 17.6 us
    all_gather x1 -> x0, waiting for transfers between devices: 127 us -> none  [on_device(): lax.all_gather(basis_out, 'dp', axis=0, tiled=True)]
    all_to_all x0 -> x1, starting transfers between devices: none -> 17.4 us  [swapped_in(): return jnp.concatenate(lax.all_to_all(repeated, name, 0, 0), axis=dim)]
    all_gather x1, waiting for transfers between devices: 124 us -> 108 us  [on_device(): full_in = lax.all_gather(basis_in, 'dp', axis=1, tiled=True)]
    all_to_all x0 -> x1, waiting for transfers between devices: none -> 14.5 us  [swapped_in(): return jnp.concatenate(lax.all_to_all(repeated, name, 0, 0), axis=dim)]
    unnamed x8 -> x7, waiting for transfers between devices: 438 us -> 437 us
where the time goes in v1:
time: 967 us
  waiting for transfers between devices  808 us (84%)
  blocking collectives  92.8 us (10%)
  starting transfers between devices  17.6 us (2%)
  matrix products  15.9 us (2%)
  between operations  15.5 us (2%)
  local copies, waits for them, and re-layouts  15.2 us (2%)
    unnamed x7, waiting for transfers between devices  437 us
    all_gather x1, waiting for transfers between devices, on_device(): full_in = lax.all_gather(basis_in, 'dp', axis=1, tiled=True)  108 us
    reduce_scatter x1, waiting for transfers between devices, on_device(): lax.psum_scatter(lax.dot_general(full_in, acts, (((0,), (1,)), ((), ())),...  91.6 us
    all_gather x1, waiting for transfers between devices, on_device(): whole_grads = lax.all_gather(grads, 'mp', axis=1, tiled=True)  81.8 us
    all_gather x1, blocking collectives, on_device(): scaled_wide = lax.all_gather(scaled, 'dp', axis=1, tiled=True)  62.7 us
    all_gather x1, waiting for transfers between devices, on_device(): piece = lax.all_gather(stacked, 'mp', axis=2, tiled=True)  50.1 us
    all_gather x1, blocking collectives, on_device(): out_rows = lax.all_gather(basis_out, 'mp', axis=1, tiled=True)  30.1 us
    all_gather x1, waiting for transfers between devices, on_device(): scaled_full = lax.all_gather(scaled_wide, 'mp', axis=0, tiled=True)  24.9 us
  transfers between devices with their start and end apart: 7, of which 7 were waited for; matrix products, arithmetic and copies ran while one was open for 2% of the time, Pallas kernels for 0%

profile of v1, /device:TPU:2, one launch (start us, length us, event | category | flops | bytes accessed | tf_op | source)
XLA Modules:
  0.0 966.7 jit_solution(13261859677522729579)
XLA Ops:
  7.2 0.0 all-gather.6.cloned.1.call-start
  7.2 0.7 all-gather.6.cloned.1.call-update
  7.9 0.0 all-gather.12.cloned.1.call-start
  8.0 0.7 all-gather.12.cloned.1.call-update
  8.7 2.6 stack.14
  11.2 17.4 %all-to-all-start = ((bf16[64,128,128]{2,1,0:T(8,128)(2,1)}), bf16[64,128,128]{2,1,0:T(8,128)(2,1)}, u32[]{:S(2)}, u32[]{:S(2)}) async-start(bf16[64,128,128]{2,1,0:T(8,128)(2,1)} %stack.14), calls=%async_computation.1 | async-start | bytes 4194304 | tf_op jit(solution)/shard_map/all_to_all | solution.py:9
  28.6 0.0 all-gather.8.cloned.1.call-start
  28.7 81.8 %all-gather.6.cloned.1.call-done = bf16[256,8192]{1,0:T(8,128)(2,1)} async-done(((bf16[256,1024]{1,0:T(8,128)(2,1)}), bf16[256,8192]{1,0:T(8,128)(2,1)}) %all-gather.6.cloned.1.call-update) | async-done | bytes 4194320 | tf_op jit(solution)/shard_map/all_gather | solution.py:15
  110.5 14.5 %all-to-all-done = bf16[64,128,128]{2,1,0:T(8,128)(2,1)} async-done(((bf16[64,128,128]{2,1,0:T(8,128)(2,1)}), bf16[64,128,128]{2,1,0:T(8,128)(2,1)}, u32[]{:S(2)}, u32[]{:S(2)}) %all-to-all-start) | async-done | bytes 2097184 | tf_op jit(solution)/shard_map/all_to_all | solution.py:9
  124.9 4.1 convolution_convert_fusion.2
  129.1 0.7 pad_maximum_fusion.1
  129.8 0.0 reduce-scatter.2.cloned.1.call-start
  129.8 108.0 %all-gather.12.cloned.1.call-done = bf16[64,10,3584]{2,1,0:T(8,128)(2,1)} async-done(((bf16[1,10,3584]{2,1,0:T(8,128)(2,1)}), bf16[64,10,3584]{2,1,0:T(8,128)(2,1)}) %all-gather.12.cloned.1.call-update) | async-done | bytes 4587536 | tf_op jit(solution)/shard_map/all_gather | solution.py:19
  237.8 8.0 reshape.13
  245.8 4.5 fusion.4
  250.3 0.0 all-reduce.3.cloned.1.call-start
  250.4 50.1 %all-gather.8.cloned.1.call-done = bf16[2,256,1024]{2,1,0:T(8,128)(2,1)} async-done(((bf16[2,256,128]{2,1,0:T(8,128)(2,1)}), bf16[2,256,1024]{2,1,0:T(8,128)(2,1)}) %all-gather.8.cloned.1.call-update) | async-done | bytes 1048592 | tf_op jit(solution)/shard_map/all_gather | solution.py:31
  300.5 91.6 %reduce-scatter.2.cloned.1.call-done = f32[80,256]{1,0:T(8,128)} async-done(((f32[640,256]{1,0:T(8,128)}), f32[80,256]{1,0:T(8,128)}) %reduce-scatter.2.cloned.1.call-update) | async-done | bytes 81936 | tf_op jit(solution)/shard_map/reduce_scatter | solution.py:20
  392.1 1.3 convolution_bitcast_fusion.1
  393.4 1.3 convolution_bitcast_fusion
  394.7 0.1 pad_maximum_fusion
  394.8 1.3 copy.14
  396.1 0.0 all-gather.10.cloned.1.call-start
  396.8 1.3 dynamic-slice
  398.7 435.8 %all-reduce.3.cloned.1.call-done = f32[2,80,1024]{1,0,2:T(2,128)} async-done(((f32[2,80,1024]{1,0,2:T(2,128)}), f32[2,80,1024]{1,0,2:T(2,128)}) %all-reduce.3.cloned.1.call-update) | async-done | bytes 655376
  834.6 0.8 dynamic-slice_multiply_fusion
  835.4 62.7 %all_gather.21 = bf16[80,1024]{0,1:T(8,128)(2,1)S(1)} all-gather(bf16[80,16]{0,1:T(8,128)(2,1)S(1)} %divide_convert_fusion), channel_id=1, replica_groups=mesh['dp'=64,'mp'=8] {'dp'}, dimensions={1}, use_global_device_ids=true | all-gather | bytes 166400 | tf_op jit(solution)/shard_map/all_gather | solution.py:40
  898.1 0.8 copy.16
  899.0 30.1 %all_gather.23 = bf16[128,1024]{1,0:T(8,128)(2,1)S(1)} all-gather(bf16[128,128]{1,0:T(8,128)(2,1)S(1)} %copy-done.1), channel_id=1, replica_groups=mesh['dp'=64,'mp'=8] {'mp'}, dimensions={1}, use_global_device_ids=true | all-gather | bytes 294912 | tf_op jit(solution)/shard_map/all_gather | solution.py:38
  929.0 24.9 %all-gather.10.cloned.1.call-done = bf16[640,1024]{1,0:T(8,128)(2,1)} async-done(((bf16[80,1024]{1,0:T(8,128)(2,1)}), bf16[640,1024]{1,0:T(8,128)(2,1)}) %all-gather.10.cloned.1.call-update) | async-done | bytes 1310736 | tf_op jit(solution)/shard_map/all_gather | solution.py:41
  953.9 4.7 fusion
  958.6 1.3 copy.17
  (12 shorter events, 0.1 us)
Async XLA Ops:
  7.2 238.6 %copy-start = (bf16[256,3584]{1,0:T(8,128)(2,1)S(1)}, bf16[256,3584]{1,0:T(8,128)(2,1)}, u32[]{:S(2)}) copy-start(bf16[256,3584]{1,0:T(8,128)(2,1)} %param.5) | copy-start | bytes 5505028
  7.2 103.3 %all-gather.6.cloned.1.call-start = ((), (), s32[]{:S(2)}) async-start(), calls=%async_computation.3 | async-start | bytes 4718592 | tf_op jit(solution)/shard_map/all_gather | solution.py:15
  7.9 229.9 %all-gather.12.cloned.1.call-start = ((), (), s32[]{:S(2)}) async-start(), calls=%async_computation.6 | async-start | bytes 7454720 | tf_op jit(solution)/shard_map/all_gather | solution.py:19
  11.2 113.7 %all-to-all-start = ((bf16[64,128,128]{2,1,0:T(8,128)(2,1)}), bf16[64,128,128]{2,1,0:T(8,128)(2,1)}, u32[]{:S(2)}, u32[]{:S(2)}) async-start(bf16[64,128,128]{2,1,0:T(8,128)(2,1)} %stack.14), calls=%async_computation.1 | async-start | bytes 4194304 | tf_op jit(solution)/shard_map/all_to_all | solution.py:9
  28.6 271.9 %all-gather.8.cloned.1.call-start = ((), (), s32[]{:S(2)}) async-start(), calls=%async_computation.4 | async-start | bytes 1179648 | tf_op jit(solution)/shard_map/all_gather | solution.py:31
  129.8 262.4 %reduce-scatter.2.cloned.1.call-start = ((), (), s32[]{:S(2)}) async-start(), calls=%async_computation.2 | async-start | bytes 737280 | tf_op jit(solution)/shard_map/reduce_scatter | solution.py:20
  250.3 584.3 %all-reduce.3.cloned.1.call-start = ((), (), s32[]{:S(2)}) async-start(), calls=%async_computation.7 | async-start | bytes 2097152
  394.8 504.2 %copy-start.1 = (bf16[128,128]{1,0:T(8,128)(2,1)S(1)}, bf16[128,128]{1,0:T(8,128)(2,1)}, u32[]{:S(2)}) copy-start(bf16[128,128]{1,0:T(8,128)(2,1)} %param.8) | copy-start | bytes 98308
  396.1 557.8 %all-gather.10.cloned.1.call-start = ((), (), s32[]{:S(2)}) async-start(), calls=%async_computation.5 | async-start | bytes 1474560 | tf_op jit(solution)/shard_map/all_gather | solution.py:41
  835.4 123.2 %copy-start.2 = (f32[1,80,16]{1,0,2:T(1,128)}, f32[1,80,16]{1,0,2:T(1,128)S(1)}, u32[]{:S(2)}) copy-start(f32[1,80,16]{1,0,2:T(1,128)S(1)} %get-tuple-element.10) | copy-start | bytes 15364
Sparse Core Ops, SparseCore 0:
  11.2 99.2 all-gather.5
  112.6 125.1 all-gather.11
  240.9 59.5 all-gather.7
  305.4 86.6 reduce-scatter.1
  396.2 438.2 all-reduce.2
  899.1 54.7 all-gather.9
